TPU v7x, 32 devices: a whole 2x2x4 slice. The times are simulated.
32 devices in a mesh: rep: 4 (over x, core), fsdp: 4 (over z), seq: 2 (over y).
Axes of the slice: x: 2, y: 2, z: 4, core: 2. Of those that a mesh axis runs over, the one named last changes fastest.
Arguments:
- tokens: bfloat16 [16, 592, 1024], P(('rep', 'fsdp'), 'seq'), may hold values from -6 to 6
- slot_mask: int32 [16], P(('rep', 'fsdp')), may hold values 0 or 1
- cotangent: bfloat16 [16, 592, 1024], P(('rep', 'fsdp'), 'seq'), may hold values from -6 to 6
- w_qkv: float32 [1024, 3072], P('fsdp'), may hold values from -0.25 to 0.25
- w_out: float32 [1024, 1024], P('fsdp'), may hold values from -0.75 to 0.75
- w_fc1: float32 [1024, 4096], P('fsdp'), may hold values from -0.1875 to 0.1875
- w_fc2: float32 [4096, 1024], P('fsdp'), may hold values from -0.125 to 0.125
- ln_gains: float32 [2, 1024], P(None, 'fsdp'), may hold values from 0.5 to 1.5
- biases: float32 [6, 1024], P(None, 'fsdp'), may hold values from -2 to 2
- fc1_bias: float32 [4096], P('fsdp'), may hold values from -2 to 2
Outputs:
- output: bfloat16 [16, 592, 1024], P(('rep', 'fsdp'), 'seq')
- grad_tokens: bfloat16 [16, 592, 1024], P(('rep', 'fsdp'), 'seq')
- grad_w_qkv: float32 [1024, 3072], P('fsdp')
- grad_w_out: float32 [1024, 1024], P('fsdp')
- grad_w_fc1: float32 [1024, 4096], P('fsdp')
- grad_w_fc2: float32 [4096, 1024], P('fsdp')
- grad_ln_gains: float32 [2, 1024], P(None, 'fsdp')
- grad_biases: float32 [6, 1024], P(None, 'fsdp')
- grad_fc1_bias: float32 [4096], P('fsdp')
All inputs are finite; a program needn't handle non-finite values. No bound on the sum of `slot_mask` on one device may be relied on, other than what follows from the above.
Results may differ from a plain program's by a relative error of at most 0.02.
The roundings to bfloat16 on the way count: a program that leaves them out, or rounds other values in their place, can miss the bound.
Values may be sent and summed in bfloat16 or wider, within the bound.
No kernel may reach another device: no remote copies, remote signals or barrier semaphores. Data moves between devices by JAX's collectives and lax.ppermute only.
A program may use at most 192 MiB of HBM per device.

v0:
```python
import jax
import jax.numpy as jnp
from jax import lax
from jax.sharding import PartitionSpec as P

HEADS = 16
HEAD_DIM = 64
IMG_TOK = 577
EPSILON = 1e-05
NEGATIVE = -1e30


def normalize(inputs, gain_row, shift_row):
    center = inputs - jnp.mean(inputs, axis=-1, keepdims=True)
    inverse = lax.rsqrt(jnp.mean(center * center, axis=-1, keepdims=True) + EPSILON)
    scaled = center * inverse
    return (scaled * gain_row + shift_row, scaled, inverse)


def norm_back(grad_in, scaled, inverse, gain_row):
    weighted = grad_in * gain_row
    return inverse * (
        weighted
        - jnp.mean(weighted, axis=-1, keepdims=True)
        - scaled * jnp.mean(weighted * scaled, axis=-1, keepdims=True)
    )


def across_rows(left_rows, right_rows):
    return lax.dot_general(
        left_rows, right_rows, (((0,), (0,)), ((), ())), preferred_element_type=jnp.float32
    )


def times_transposed(left_rows, right_rows):
    return lax.dot_general(
        left_rows, right_rows, (((1,), (1,)), ((), ())), preferred_element_type=jnp.float32
    )


def split_heads(matrix):
    return matrix.reshape(matrix.shape[0], HEADS, HEAD_DIM)


def masked_scores(query_rows, key_rows):
    scores = jnp.einsum(
        "qhd,khd->hqk",
        split_heads(query_rows),
        split_heads(key_rows),
        preferred_element_type=jnp.float32,
    )
    valid_keys = jnp.arange(key_rows.shape[0]) < IMG_TOK
    return jnp.where(valid_keys[None, None, :], scores, NEGATIVE)


def attend_slot(blocks_in):
    query_rows, key_rows, value_rows = blocks_in
    scores = masked_scores(query_rows, key_rows)
    highest = jnp.max(scores, axis=-1, keepdims=True)
    exponent = jnp.exp(scores - highest)
    total_sum = jnp.sum(exponent, axis=-1, keepdims=True)
    weights = (exponent / total_sum).astype(jnp.bfloat16)
    mixed_rows = jnp.einsum(
        "hqk,khd->qhd", weights, split_heads(value_rows), preferred_element_type=jnp.float32
    )
    return (mixed_rows.reshape(query_rows.shape[0], -1), highest + jnp.log(total_sum))


def attend_back(blocks_in):
    query_rows, key_rows, value_rows, log_total, grad_rows = blocks_in
    scores = masked_scores(query_rows, key_rows)
    probability = jnp.exp(scores - log_total)
    grad_heads = split_heads(grad_rows)
    grad_probs = jnp.einsum(
        "qhd,khd->hqk", grad_heads, split_heads(value_rows), preferred_element_type=jnp.float32
    )
    inner_sum = jnp.sum(probability * grad_probs, axis=-1, keepdims=True)
    grad_scores = (probability * (grad_probs - inner_sum)).astype(jnp.bfloat16)
    grad_query = jnp.einsum(
        "hqk,khd->qhd", grad_scores, split_heads(key_rows), preferred_element_type=jnp.float32
    )
    grad_key = jnp.einsum(
        "hqk,qhd->khd", grad_scores, split_heads(query_rows), preferred_element_type=jnp.float32
    )
    grad_value = jnp.einsum(
        "hqk,qhd->khd",
        probability.astype(jnp.bfloat16),
        grad_heads,
        preferred_element_type=jnp.float32,
    )
    key_count = key_rows.shape[0]
    return (
        grad_query.reshape(query_rows.shape[0], -1),
        grad_key.reshape(key_count, -1),
        grad_value.reshape(key_count, -1),
    )


def on_device(tokens, slot_mask, cotangent, w_qkv, w_out, w_fc1, w_fc2, ln_gains, biases, fc1_bias):
    slot_count, row_count, feature_width = tokens.shape
    low_qkv = w_qkv.astype(jnp.bfloat16)
    low_out = w_out.astype(jnp.bfloat16)
    low_fc1 = w_fc1.astype(jnp.bfloat16)
    low_fc2 = w_fc2.astype(jnp.bfloat16)
    low_gains = ln_gains.astype(jnp.bfloat16)
    low_biases = biases.astype(jnp.bfloat16)
    low_fc1_bias = fc1_bias.astype(jnp.bfloat16)
    gathered = (
        lax.all_gather(low_qkv, "fsdp", axis=0, tiled=True),
        lax.all_gather(low_out, "fsdp", axis=0, tiled=True),
        lax.all_gather(low_fc1, "fsdp", axis=0, tiled=True),
        lax.all_gather(low_fc2, "fsdp", axis=0, tiled=True),
        lax.all_gather(low_gains, "fsdp", axis=1, tiled=True),
        lax.all_gather(low_biases, "fsdp", axis=1, tiled=True),
        lax.all_gather(low_fc1_bias, "fsdp", axis=0, tiled=True),
    )
    big_qkv, big_out, big_fc1, big_fc2, gain_rows, bias_rows, fc1_shift = gathered
    gain_values = gain_rows.astype(jnp.float32)
    shift_values = bias_rows.astype(jnp.float32)
    hidden_shift = fc1_shift.astype(jnp.float32)
    head_scale = HEAD_DIM ** (-0.5)
    positions = lax.axis_index("seq") * row_count + jnp.arange(row_count)
    keep_mask = (
        slot_mask.astype(jnp.float32)[:, None] * (positions < IMG_TOK).astype(jnp.float32)[None, :]
    )
    keep_mask = keep_mask.reshape(-1, 1)
    inputs = tokens.astype(jnp.float32).reshape(-1, feature_width)
    normed_full, scaled_one, inverse_one = normalize(inputs, gain_values[0], shift_values[0])
    normed = normed_full.astype(jnp.bfloat16)
    joined = jnp.dot(normed, big_qkv, preferred_element_type=jnp.float32)
    queries = ((joined[:, :feature_width] + shift_values[1]) * head_scale).astype(jnp.bfloat16)
    keys_local = (
        joined[:, feature_width : 2 * feature_width]
        .astype(jnp.bfloat16)
        .reshape(slot_count, row_count, feature_width)
    )
    values_local = (
        (joined[:, 2 * feature_width :] + shift_values[2])
        .astype(jnp.bfloat16)
        .reshape(slot_count, row_count, feature_width)
    )
    slot_queries = queries.reshape(slot_count, row_count, feature_width)
    keys_all, values_all = (
        lax.all_gather(keys_local, "seq", axis=1, tiled=True),
        lax.all_gather(values_local, "seq", axis=1, tiled=True),
    )
    mixed_rows, log_total = lax.map(attend_slot, (slot_queries, keys_all, values_all))
    mixed_low = mixed_rows.reshape(-1, feature_width).astype(jnp.bfloat16)
    middle = inputs + (
        jnp.dot(mixed_low, big_out, preferred_element_type=jnp.float32) + shift_values[3]
    )
    normed_two_full, scaled_two, inverse_two = normalize(middle, gain_values[1], shift_values[4])
    normed_two = normed_two_full.astype(jnp.bfloat16)
    hidden = jnp.dot(normed_two, big_fc1, preferred_element_type=jnp.float32) + hidden_shift
    gate_values = jax.nn.sigmoid(1.702 * hidden)
    active = (hidden * gate_values).astype(jnp.bfloat16)
    result = jnp.dot(active, big_fc2, preferred_element_type=jnp.float32) + shift_values[5]
    output = ((middle + result) * keep_mask).astype(jnp.bfloat16).reshape(tokens.shape)
    again = (
        lax.all_gather(low_qkv, "fsdp", axis=0, tiled=True),
        lax.all_gather(low_out, "fsdp", axis=0, tiled=True),
        lax.all_gather(low_fc1, "fsdp", axis=0, tiled=True),
        lax.all_gather(low_fc2, "fsdp", axis=0, tiled=True),
        lax.all_gather(low_gains, "fsdp", axis=1, tiled=True),
        lax.all_gather(low_biases, "fsdp", axis=1, tiled=True),
        lax.all_gather(low_fc1_bias, "fsdp", axis=0, tiled=True),
    )
    back_qkv, back_out, back_fc1, back_fc2, back_gain_rows = (
        again[0],
        again[1],
        again[2],
        again[3],
        again[4],
    )
    back_gains = back_gain_rows.astype(jnp.float32)
    incoming = cotangent.astype(jnp.float32).reshape(-1, feature_width) * keep_mask
    grad_result = incoming.astype(jnp.bfloat16)
    grad_fc2 = across_rows(active, grad_result)
    grad_shift_five = jnp.sum(grad_result.astype(jnp.float32), axis=0)
    grad_active = times_transposed(grad_result, back_fc2)
    grad_hidden = (
        grad_active * (gate_values + 1.702 * hidden * gate_values * (1.0 - gate_values))
    ).astype(jnp.bfloat16)
    grad_fc1 = across_rows(normed_two, grad_hidden)
    grad_hidden_shift = jnp.sum(grad_hidden.astype(jnp.float32), axis=0)
    grad_normed_two = times_transposed(grad_hidden, back_fc1)
    grad_gain_two = jnp.sum(grad_normed_two * scaled_two, axis=0)
    grad_shift_four = jnp.sum(grad_normed_two, axis=0)
    grad_middle = incoming + norm_back(grad_normed_two, scaled_two, inverse_two, back_gains[1])
    grad_branch = grad_middle.astype(jnp.bfloat16)
    grad_out = across_rows(mixed_low, grad_branch)
    grad_shift_three = jnp.sum(grad_branch.astype(jnp.float32), axis=0)
    grad_mixed = times_transposed(grad_branch, back_out).astype(jnp.bfloat16)
    grad_query, key_part, value_part = lax.map(
        attend_back,
        (
            slot_queries,
            keys_all,
            values_all,
            log_total,
            grad_mixed.reshape(slot_count, row_count, feature_width),
        ),
    )
    grad_keys, grad_values = (
        lax.psum_scatter(
            key_part.astype(jnp.bfloat16), "seq", scatter_dimension=1, tiled=True
        ).astype(jnp.float32),
        lax.psum_scatter(
            value_part.astype(jnp.bfloat16), "seq", scatter_dimension=1, tiled=True
        ).astype(jnp.float32),
    )
    query_grad_low = (grad_query.astype(jnp.bfloat16) * head_scale).reshape(-1, feature_width)
    key_grad_low = grad_keys.astype(jnp.bfloat16).reshape(-1, feature_width)
    value_grad_low = grad_values.astype(jnp.bfloat16).reshape(-1, feature_width)
    grad_joined = jnp.concatenate([query_grad_low, key_grad_low, value_grad_low], axis=1)
    grad_qkv = across_rows(normed, grad_joined)
    grad_shift_one = jnp.sum(query_grad_low.astype(jnp.float32), axis=0)
    grad_shift_two = jnp.sum(value_grad_low.astype(jnp.float32), axis=0)
    grad_normed = times_transposed(grad_joined, back_qkv)
    grad_gain_one = jnp.sum(grad_normed * scaled_one, axis=0)
    grad_shift_zero = jnp.sum(grad_normed, axis=0)
    grad_inputs = grad_middle + norm_back(grad_normed, scaled_one, inverse_one, back_gains[0])
    grad_tokens = grad_inputs.astype(jnp.bfloat16).reshape(tokens.shape)
    grad_gains = jnp.stack([grad_gain_one, grad_gain_two])
    grad_shifts = jnp.stack(
        [
            grad_shift_zero,
            grad_shift_one,
            grad_shift_two,
            grad_shift_three,
            grad_shift_four,
            grad_shift_five,
        ]
    )
    shards = (
        lax.psum_scatter(
            grad_qkv.astype(jnp.bfloat16), "fsdp", scatter_dimension=0, tiled=True
        ).astype(jnp.float32),
        lax.psum_scatter(
            grad_out.astype(jnp.bfloat16), "fsdp", scatter_dimension=0, tiled=True
        ).astype(jnp.float32),
        lax.psum_scatter(
            grad_fc1.astype(jnp.bfloat16), "fsdp", scatter_dimension=0, tiled=True
        ).astype(jnp.float32),
        lax.psum_scatter(
            grad_fc2.astype(jnp.bfloat16), "fsdp", scatter_dimension=0, tiled=True
        ).astype(jnp.float32),
        lax.psum_scatter(
            grad_gains.astype(jnp.bfloat16), "fsdp", scatter_dimension=1, tiled=True
        ).astype(jnp.float32),
        lax.psum_scatter(
            grad_shifts.astype(jnp.bfloat16), "fsdp", scatter_dimension=1, tiled=True
        ).astype(jnp.float32),
        lax.psum_scatter(
            grad_hidden_shift.astype(jnp.bfloat16), "fsdp", scatter_dimension=0, tiled=True
        ).astype(jnp.float32),
    )
    summed = (
        lax.psum(shards[0].astype(jnp.bfloat16), ("rep", "seq")).astype(jnp.float32),
        lax.psum(shards[1].astype(jnp.bfloat16), ("rep", "seq")).astype(jnp.float32),
        lax.psum(shards[2].astype(jnp.bfloat16), ("rep", "seq")).astype(jnp.float32),
        lax.psum(shards[3].astype(jnp.bfloat16), ("rep", "seq")).astype(jnp.float32),
        lax.psum(shards[4].astype(jnp.bfloat16), ("rep", "seq")).astype(jnp.float32),
        lax.psum(shards[5].astype(jnp.bfloat16), ("rep", "seq")).astype(jnp.float32),
        lax.psum(shards[6].astype(jnp.bfloat16), ("rep", "seq")).astype(jnp.float32),
    )
    return (
        output,
        grad_tokens,
        summed[0],
        summed[1],
        summed[2],
        summed[3],
        summed[4],
        summed[5],
        summed[6],
    )


def solution(mesh):
    return jax.shard_map(
        on_device,
        mesh=mesh,
        in_specs=(
            P(("rep", "fsdp"), "seq", None),
            P(("rep", "fsdp")),
            P(("rep", "fsdp"), "seq", None),
            P("fsdp", None),
            P("fsdp", None),
            P("fsdp", None),
            P("fsdp", None),
            P(None, "fsdp"),
            P(None, "fsdp"),
            P("fsdp"),
        ),
        out_specs=(
            P(("rep", "fsdp"), "seq", None),
            P(("rep", "fsdp"), "seq", None),
            P("fsdp", None),
            P("fsdp", None),
            P("fsdp", None),
            P("fsdp", None),
            P(None, "fsdp"),
            P(None, "fsdp"),
            P("fsdp"),
        ),
        check_vma=False,
    )
```

profile of v0, /device:TPU:0, one launch (start us, length us, event | category | flops | bytes accessed | tf_op | source)
XLA Modules:
  0.0 1236.4 jit_solution(1024592312134364579)
XLA Ops:
  7.3 3.3 convert_element_type.215
  10.7 12.6 %all_gather.32 = bf16[2,1024]{1,0:T(2,128)(2,1)S(1)} all-gather(bf16[2,256]{1,0:T(2,128)(2,1)S(1)} %convert_element_type.210), channel_id=1, replica_groups=mesh['rep'=4,'fsdp'=4,'seq'=2] {'fsdp'}, dimensions={1}, use_global_device_ids=true | all-gather | bytes 5120 | tf_op jit(solution)/shard_map/all_gather | solution.py:113
  23.3 14.3 %all_gather.33 = bf16[6,1024]{1,0:T(8,128)(2,1)S(1)} all-gather(bf16[6,256]{1,0:T(8,128)(2,1)S(1)} %convert_element_type.212), channel_id=1, replica_groups=mesh['rep'=4,'fsdp'=4,'seq'=2] {'fsdp'}, dimensions={1}, use_global_device_ids=true | all-gather | bytes 15360 | tf_op jit(solution)/shard_map/all_gather | solution.py:114
  38.1 90.8 %all-gather.9.cloned.1.call-done = bf16[1024,3072]{1,0:T(8,128)(2,1)} async-done(((bf16[256,3072]{1,0:T(8,128)(2,1)}), bf16[1024,3072]{1,0:T(8,128)(2,1)}) %all-gather.9.cloned.1.call-update) | async-done | bytes 6291472 | tf_op jit(solution)/shard_map/all_gather | solution.py:109
  128.9 5.0 fusion.53
  134.0 1.8 copy-done.8
  135.8 0.9 slice.67
  136.8 2.9 fusion.36
  139.7 0.9 convert_element_type.222
  140.7 4.1 convert_element_type.224
  144.9 3.8 convert_element_type.228
  149.5 11.9 all_gather.39
  161.8 1.9 copy.33
  163.7 19.9 %all-gather.17.cloned.1.call-done = bf16[592,1024]{1,0:T(8,128)(2,1)} async-done(((bf16[296,1024]{1,0:T(8,128)(2,1)}), bf16[592,1024]{1,0:T(8,128)(2,1)}) %all-gather.17.cloned.1.call-update) | async-done | bytes 1212432 | tf_op jit(solution)/shard_map/all_gather | solution.py:145
  183.6 2.4 copy.31
  186.0 2.2 select_reduce_fusion
  188.2 3.2 fusion
  191.5 1.7 copy-done
  193.1 4.5 fusion.20
  197.6 33.4 %all-gather.11.cloned.1.call-done = bf16[1024,1024]{1,0:T(8,128)(2,1)} async-done(((bf16[256,1024]{1,0:T(8,128)(2,1)}), bf16[1024,1024]{1,0:T(8,128)(2,1)}) %all-gather.11.cloned.1.call-update) | async-done | bytes 2097168 | tf_op jit(solution)/shard_map/all_gather | solution.py:110
  231.0 2.8 fusion.59
  234.1 147.3 %all-gather.13.cloned.1.call-done = bf16[1024,4096]{1,0:T(8,128)(2,1)} async-done(((bf16[256,4096]{1,0:T(8,128)(2,1)}), bf16[1024,4096]{1,0:T(8,128)(2,1)}) %all-gather.13.cloned.1.call-update) | async-done | bytes 8388624 | tf_op jit(solution)/shard_map/all_gather | solution.py:111
  381.4 8.5 convolution_add_fusion
  389.9 141.4 %all-gather.15.cloned.1.call-done = bf16[4096,1024]{1,0:T(8,128)(2,1)} async-done(((bf16[1024,1024]{1,0:T(8,128)(2,1)}), bf16[4096,1024]{1,0:T(8,128)(2,1)}) %all-gather.15.cloned.1.call-update) | async-done | bytes 8388624 | tf_op jit(solution)/shard_map/all_gather | solution.py:112
  531.3 9.1 fusion.61
  540.4 3.1 multiply_reduce_fusion.1
  544.1 1.0 copy-done.3
  545.1 1.7 convolution_convert_fusion.6
  546.8 2.2 copy.34
  549.0 8.5 fusion.9
  557.6 6.2 copy.37
  563.8 3.2 copy.46
  567.0 9.8 multiply_reduce_fusion
  576.8 6.6 multiply_convert_fusion
  583.4 2.9 convolution_convert_fusion.4
  586.4 6.2 copy.35
  592.6 3.1 copy.47
  595.8 4.1 convolution_convert_fusion.3
  600.4 5.6 fusion.60
  606.0 2.7 fusion.56
  608.7 2.2 copy.38
  610.9 5.2 reduce-scatter.25.cloned.1.call-done
  616.0 1.7 reshape_bitcast_fusion.1
  617.7 2.2 copy.36
  620.0 7.4 convolution_convert_fusion.2
  627.4 1.0 copy-done.15
  628.4 9.7 convolution_convert_fusion
  638.1 8.8 convolution_convert_fusion.1
  647.2 6.6 fusion.33
  655.7 7.2 reduce-scatter.17.cloned.1.call-done
  662.8 112.4 %reduce-scatter.15.cloned.1.call-done = bf16[256,3072]{1,0:T(8,128)(2,1)} async-done(((bf16[1024,3072]{1,0:T(8,128)(2,1)}), bf16[256,3072]{1,0:T(8,128)(2,1)}) %reduce-scatter.15.cloned.1.call-update) | async-done | bytes 1572880 | tf_op jit(solution)/shard_map/reduce_scatter | solution.py:236
  775.2 147.5 %reduce-scatter.21.cloned.1.call-done = bf16[1024,1024]{1,0:T(8,128)(2,1)} async-done(((bf16[4096,1024]{1,0:T(8,128)(2,1)}), bf16[1024,1024]{1,0:T(8,128)(2,1)}) %reduce-scatter.21.cloned.1.call-update) | async-done | bytes 2097168 | tf_op jit(solution)/shard_map/reduce_scatter | solution.py:245
  922.7 147.6 %reduce-scatter.19.cloned.1.call-done = bf16[256,4096]{1,0:T(8,128)(2,1)} async-done(((bf16[1024,4096]{1,0:T(8,128)(2,1)}), bf16[256,4096]{1,0:T(8,128)(2,1)}) %reduce-scatter.19.cloned.1.call-update) | async-done | bytes 2097168 | tf_op jit(solution)/shard_map/reduce_scatter | solution.py:242
  1072.1 11.4 all-reduce
  1083.6 8.6 fusion.25
  1092.2 1.3 fusion.41
  1093.5 0.9 copy.40
  1094.5 18.9 %reduce-scatter.23.cloned.1.call-done = bf16[6,256]{1,0:T(8,128)(2,1)} async-done(((bf16[6,1024]{1,0:T(8,128)(2,1)}), bf16[6,256]{1,0:T(8,128)(2,1)}) %reduce-scatter.23.cloned.1.call-update) | async-done | bytes 3088 | tf_op jit(solution)/shard_map/reduce_scatter | solution.py:251
  1113.4 14.1 %all-reduce.1 = (bf16[2,256]{1,0:T(2,128)(2,1)S(1)}, bf16[6,256]{1,0:T(8,128)(2,1)S(1)}, bf16[1024]{0:T(1024)(128)(2,1)S(1)}) all-reduce(bf16[2,256]{1,0:T(2,128)(2,1)S(1)} %copy.40, bf16[6,256]{1,0:T(8,128)(2,1)} %reduce-scatter.23.cloned.1.call-done, ...), channel_id=1, replica_groups=mesh['rep'=4,'fsdp'=4,'seq'=2] {'rep','seq'}, use_global_device_ids=true, to_apply=%region_24.25 | all-reduce | flops 3072 | bytes 12288 | tf_op jit(solution)/shard_map/psum | solution.py:263
  1129.2 91.0 %all-reduce.5.cloned.1.call-done = (bf16[256,3072]{1,0:T(8,128)(2,1)}, bf16[256,1024]{1,0:T(8,128)(2,1)}, bf16[256,4096]{1,0:T(8,128)(2,1)}, bf16[1024,1024]{1,0:T(8,128)(2,1)}) async-done(((bf16[256,3072]{1,0:T(8,128)(2,1)}, bf16[256,1024]{1,0:T(8,128)(2,1)}, bf16[256,4096]{1,0:T(8,128)(2,1)}, bf16[1024,1024]{1,0:T(8,128)(2,1)}), (bf16[256,3072]{1,0:T(8,128)(2,1)}, bf16[256,1024]{1,0:T(8,128)(2,1)}, ...) | async-done | bytes 6291472 | tf_op jit(solution)/shard_map/psum | solution.py:259
  1220.3 2.2 convert_element_type.248
  1222.5 2.0 convert_element_type.246
  1224.7 2.5 convert_element_type.250
  1227.2 2.5 convert_element_type.252
  (113 shorter events, 8.3 us)
Async XLA Ops:
  7.2 3.5 copy-start.19
  7.2 3.5 copy-start.17
  7.2 30.4 %copy-start.2 = (bf16[1,296,1024]{2,1,0:T(8,128)(2,1)S(1)}, bf16[1,296,1024]{2,1,0:T(8,128)(2,1)}, u32[]{:S(2)}) copy-start(bf16[1,296,1024]{2,1,0:T(8,128)(2,1)} %param.10) | copy-start | bytes 1818628
  7.2 121.7 %all-gather.9.cloned.1.call-start = ((), (), s32[]{:S(2)}) async-start(), calls=%async_computation.8 | async-start | bytes 7864320 | tf_op jit(solution)/shard_map/all_gather | solution.py:109
  10.6 151.2 %all-gather.19.cloned.1.call-start = ((), (), s32[]{:S(2)}) async-start(), calls=%async_computation.18 | async-start | bytes 1818624 | tf_op jit(solution)/shard_map/all_gather | solution.py:144
  134.0 1.8 copy-start.8
  136.7 46.9 %all-gather.17.cloned.1.call-start = ((), (), s32[]{:S(2)}) async-start(), calls=%async_computation.17 | async-start | bytes 1818624 | tf_op jit(solution)/shard_map/all_gather | solution.py:145
  136.8 3.0 copy-start.13
  139.7 91.3 %all-gather.11.cloned.1.call-start = ((), (), s32[]{:S(2)}) async-start(), calls=%async_computation.9 | async-start | bytes 2621440 | tf_op jit(solution)/shard_map/all_gather | solution.py:110
  140.7 240.7 %all-gather.13.cloned.1.call-start = ((), (), s32[]{:S(2)}) async-start(), calls=%async_computation.10 | async-start | bytes 10485760 | tf_op jit(solution)/shard_map/all_gather | solution.py:111
  144.8 386.4 %all-gather.15.cloned.1.call-start = ((), (), s32[]{:S(2)}) async-start(), calls=%async_computation.11 | async-start | bytes 10485760 | tf_op jit(solution)/shard_map/all_gather | solution.py:112
  148.7 0.7 copy-start.18
  148.7 457.3 %reduce-scatter.27.cloned.1.call-start = ((), (), s32[]{:S(2)}) async-start(), calls=%async_computation.20 | async-start | bytes 1818624
  161.7 24.3 %copy-start.5 = (bf16[296,1024]{0,1:T(8,128)(2,1)}, bf16[296,1024]{0,1:T(8,128)(2,1)S(1)}, u32[]{:S(2)}) copy-start(bf16[296,1024]{0,1:T(8,128)(2,1)S(1)} %copy.32) | copy-start | bytes 1818628
  188.2 4.9 copy-start
  188.2 4.9 copy-start.7
  531.3 9.1 copy-start.20
  540.3 3.1 copy-start.22
  540.3 3.1 copy-start.14
  543.5 1.6 copy-start.11
  544.1 1.0 copy-start.3
  567.0 49.1 %reduce-scatter.25.cloned.1.call-start = ((), (), s32[]{:S(2)}) async-start(), calls=%async_computation.19 | async-start | bytes 1818624
  576.8 6.6 copy-start.6
  583.4 3.0 copy-start.1
  595.8 67.0 %reduce-scatter.17.cloned.1.call-start = ((), (), s32[]{:S(2)}) async-start(), calls=%async_computation.13 | async-start | bytes 2621440 | tf_op jit(solution)/shard_map/reduce_scatter | solution.py:239
  600.0 175.2 %reduce-scatter.15.cloned.1.call-start = ((), (), s32[]{:S(2)}) async-start(), calls=%async_computation.12 | async-start | bytes 7864320 | tf_op jit(solution)/shard_map/reduce_scatter | solution.py:236
  627.3 1.1 copy-start.15
  627.4 295.3 %reduce-scatter.21.cloned.1.call-start = ((), (), s32[]{:S(2)}) async-start(), calls=%async_computation.15 | async-start | bytes 10485760 | tf_op jit(solution)/shard_map/reduce_scatter | solution.py:245
  638.1 432.1 %reduce-scatter.19.cloned.1.call-start = ((), (), s32[]{:S(2)}) async-start(), calls=%async_computation.14 | async-start | bytes 10485760 | tf_op jit(solution)/shard_map/reduce_scatter | solution.py:242
  647.0 446.6 %reduce-scatter.29.cloned.1.call-start = ((), (), s32[]{:S(2)}) async-start(), calls=%async_computation.21 | async-start | bytes 327680
  654.7 458.6 %reduce-scatter.23.cloned.1.call-start = ((), (), s32[]{:S(2)}) async-start(), calls=%async_computation.16 | async-start | bytes 20480 | tf_op jit(solution)/shard_map/reduce_scatter | solution.py:251
  655.6 564.7 %all-reduce.5.cloned.1.call-start = ((), (), s32[]{:S(2)}) async-start(), calls=%async_computation.22 | async-start | bytes 12582912 | tf_op jit(solution)/shard_map/psum | solution.py:259
  1070.2 0.7 copy-start.21
  1083.5 8.7 copy-start.16
  1083.5 8.7 copy-start.4
  1092.2 21.2 %dynamic-slice-start = ((bf16[4096]{0:T(1024)(128)(2,1)}, u32[]{:T(128)}), bf16[1024]{0:T(1024)(128)(2,1)S(1)}, s32[]{:S(2)}) async-start(bf16[4096]{0:T(1024)(128)(2,1)} %copy-done.16, u32[]{:T(128)} %multiply.49), calls=%async_computation.23 | async-start | bytes 4608
  1220.3 2.2 copy-start.12
  1222.5 2.2 copy-start.10
  1224.7 2.5 copy-start.9
Sparse Core Ops, SparseCore 0:
  10.7 118.1 all-gather.8
  136.8 21.4 all-gather.18
  160.4 23.1 all-gather.16
  185.0 45.9 all-gather.10
  233.0 148.3 all-gather.12
  383.4 147.8 all-gather.14
  567.1 20.3 reduce-scatter.26
  595.9 20.0 reduce-scatter.24
  618.9 43.8 reduce-scatter.16
  665.1 110.0 reduce-scatter.14
  777.6 144.9 reduce-scatter.20
  925.0 145.1 reduce-scatter.18
  1073.2 20.3 reduce-scatter.28
  1096.2 17.1 reduce-scatter.22
  1117.3 102.9 all-reduce.4
where the time goes:
time: 1240 us
  waiting for transfers between devices  963 us (78%)
  matrix products  109 us (9%)
  blocking collectives  64.3 us (5%)
  local copies, waits for them, and re-layouts  42.4 us (3%)
  other arithmetic  41.2 us (3%)
  between operations  15.9 us (1%)
    reduce_scatter x1, waiting for transfers between devices, on_device(): lax.psum_scatter(grad_fc1.astype(jnp.bfloat16), 'fsdp', scatter_dimension...  148 us
    reduce_scatter x1, waiting for transfers between devices, on_device(): lax.psum_scatter(grad_fc2.astype(jnp.bfloat16), 'fsdp', scatter_dimension...  148 us
    all_gather x1, waiting for transfers between devices, on_device(): lax.all_gather(low_fc1, 'fsdp', axis=0, tiled=True)  147 us
    all_gather x1, waiting for transfers between devices, on_device(): lax.all_gather(low_fc2, 'fsdp', axis=0, tiled=True)  141 us
    reduce_scatter x1, waiting for transfers between devices, on_device(): lax.psum_scatter(grad_qkv.astype(jnp.bfloat16), 'fsdp', scatter_dimension...  112 us
    psum x1, waiting for transfers between devices, on_device(): lax.psum(shards[0].astype(jnp.bfloat16), ('rep', 'seq')).astype(jnp.float32)  91 us
    all_gather x1, waiting for transfers between devices, on_device(): lax.all_gather(low_qkv, 'fsdp', axis=0, tiled=True)  90.8 us
    unnamed x58, local copies, waits for them, and re-layouts  33.7 us
  transfers between devices with their start and end apart: 15, of which 12 were waited for; matrix products, arithmetic and copies ran while one was open for 11% of the time, Pallas kernels for 0%

commit v1 on v0

--- a/solution.py
+++ b/solution.py
@@ -256,7 +256,7 @@
         ).astype(jnp.float32),
     )
     summed = (
-        lax.psum(shards[0].astype(jnp.bfloat16), ("rep", "seq")).astype(jnp.float32),
+        lax.psum(lax.psum(shards[0].astype(jnp.bfloat16), "seq"), "rep").astype(jnp.float32),
         lax.psum(shards[1].astype(jnp.bfloat16), ("rep", "seq")).astype(jnp.float32),
         lax.psum(shards[2].astype(jnp.bfloat16), ("rep", "seq")).astype(jnp.float32),
         lax.psum(shards[3].astype(jnp.bfloat16), ("rep", "seq")).astype(jnp.float32),

time: 1240 us -> 1330 us (1.073)
  waiting for transfers between devices: 963 us -> 1050 us
    psum x1 -> x3, waiting for transfers between devices: 91 us -> 136 us  [the longest x1 87.3 us: on_device(): lax.psum(shards[1].astype(jnp.bfloat16), ('rep', 'seq')).astype(jnp.float32)]
    reduce_scatter x1, waiting for transfers between devices: 7.15 us -> 46.8 us  [on_device(): lax.psum_scatter(grad_out.astype(jnp.bfloat16), 'fsdp', scatter_dimension...]
    all_gather x1, waiting for transfers between devices: 19.9 us -> 0.02 us  [on_device(): lax.all_gather(values_local, 'seq', axis=1, tiled=True)]
    all_gather x1, waiting for transfers between devices: 0.02 us -> 19.8 us  [on_device(): lax.all_gather(keys_local, 'seq', axis=1, tiled=True)]
    unnamed x58 -> x54, local copies, waits for them, and re-layouts: 33.7 us -> 32.8 us
  transfers between devices with their start and end apart: 15 -> 17, of which waited for: 12 -> 14; matrix products, arithmetic and copies ran while one was open for 11% -> 10% of each run, Pallas kernels for 0% -> 0%
where the time goes in v1:
time: 1330 us
  waiting for transfers between devices  1050 us (79%)
  matrix products  110 us (8%)
  blocking collectives  64.3 us (5%)
  local copies, waits for them, and re-layouts  42.8 us (3%)
  other arithmetic  42.5 us (3%)
  between operations  15.9 us (1%)
    reduce_scatter x1, waiting for transfers between devices, on_device(): lax.psum_scatter(grad_fc2.astype(jnp.bfloat16), 'fsdp', scatter_dimension...  148 us
    all_gather x1, waiting for transfers between devices, on_device(): lax.all_gather(low_fc1, 'fsdp', axis=0, tiled=True)  147 us
    reduce_scatter x1, waiting for transfers between devices, on_device(): lax.psum_scatter(grad_fc1.astype(jnp.bfloat16), 'fsdp', scatter_dimension...  146 us
    all_gather x1, waiting for transfers between devices, on_device(): lax.all_gather(low_fc2, 'fsdp', axis=0, tiled=True)  141 us
    reduce_scatter x1, waiting for transfers between devices, on_device(): lax.psum_scatter(grad_qkv.astype(jnp.bfloat16), 'fsdp', scatter_dimension...  111 us
    all_gather x1, waiting for transfers between devices, on_device(): lax.all_gather(low_qkv, 'fsdp', axis=0, tiled=True)  90.8 us
    psum x1, waiting for transfers between devices, on_device(): lax.psum(shards[1].astype(jnp.bfloat16), ('rep', 'seq')).astype(jnp.float32)  87.3 us
    reduce_scatter x1, waiting for transfers between devices, on_device(): lax.psum_scatter(grad_out.astype(jnp.bfloat16), 'fsdp', scatter_dimension...  46.8 us
  transfers between devices with their start and end apart: 17, of which 14 were waited for; matrix products, arithmetic and copies ran while one was open for 10% of the time, Pallas kernels for 0%

profile of v1, /device:TPU:0, one launch (start us, length us, event | category | flops | bytes accessed | tf_op | source)
XLA Modules:
  0.0 1325.9 jit_solution(14956507997004816215)
XLA Ops:
  7.3 3.3 convert_element_type.215
  10.7 12.6 all_gather.32
  23.3 14.3 %all_gather.33 = bf16[6,1024]{1,0:T(8,128)(2,1)S(1)} all-gather(bf16[6,256]{1,0:T(8,128)(2,1)S(1)} %convert_element_type.212), channel_id=1, replica_groups=mesh['rep'=4,'fsdp'=4,'seq'=2] {'fsdp'}, dimensions={1}, use_global_device_ids=true | all-gather | bytes 15360 | tf_op jit(solution)/shard_map/all_gather | solution.py:114
  38.1 90.8 %all-gather.9.cloned.1.call-done = bf16[1024,3072]{1,0:T(8,128)(2,1)} async-done(((bf16[256,3072]{1,0:T(8,128)(2,1)}), bf16[1024,3072]{1,0:T(8,128)(2,1)}) %all-gather.9.cloned.1.call-update) | async-done | bytes 6291472 | tf_op jit(solution)/shard_map/all_gather | solution.py:109
  128.9 5.0 fusion.53
  134.0 1.8 copy-done.8
  135.8 1.1 fusion.36
  137.0 2.3 slice.67
  140.3 4.1 convert_element_type.224
  144.5 3.8 convert_element_type.228
  149.0 11.9 all_gather.39
  161.3 2.7 copy.31
  164.0 19.8 %all-gather.19.cloned.1.call-done = bf16[592,1024]{1,0:T(8,128)(2,1)} async-done(((bf16[296,1024]{1,0:T(8,128)(2,1)}), bf16[592,1024]{1,0:T(8,128)(2,1)}) %all-gather.19.cloned.1.call-update) | async-done | bytes 1212432 | tf_op jit(solution)/shard_map/all_gather | solution.py:144
  183.8 1.7 copy.33
  185.5 2.2 select_reduce_fusion
  187.8 3.2 fusion
  191.0 1.6 copy-done
  192.6 4.5 fusion.20
  197.1 34.1 %all-gather.11.cloned.1.call-done = bf16[1024,1024]{1,0:T(8,128)(2,1)} async-done(((bf16[256,1024]{1,0:T(8,128)(2,1)}), bf16[1024,1024]{1,0:T(8,128)(2,1)}) %all-gather.11.cloned.1.call-update) | async-done | bytes 2097168 | tf_op jit(solution)/shard_map/all_gather | solution.py:110
  231.2 2.8 fusion.59
  234.3 147.1 %all-gather.13.cloned.1.call-done = bf16[1024,4096]{1,0:T(8,128)(2,1)} async-done(((bf16[256,4096]{1,0:T(8,128)(2,1)}), bf16[1024,4096]{1,0:T(8,128)(2,1)}) %all-gather.13.cloned.1.call-update) | async-done | bytes 8388624 | tf_op jit(solution)/shard_map/all_gather | solution.py:111
  381.5 8.6 convolution_add_fusion
  390.1 141.3 %all-gather.15.cloned.1.call-done = bf16[4096,1024]{1,0:T(8,128)(2,1)} async-done(((bf16[1024,1024]{1,0:T(8,128)(2,1)}), bf16[4096,1024]{1,0:T(8,128)(2,1)}) %all-gather.15.cloned.1.call-update) | async-done | bytes 8388624 | tf_op jit(solution)/shard_map/all_gather | solution.py:112
  531.4 9.1 fusion.61
  540.5 3.1 multiply_reduce_fusion.1
  544.2 1.0 copy-done.3
  545.2 1.7 convolution_convert_fusion.6
  546.9 2.2 copy.34
  549.1 8.6 fusion.9
  557.7 6.2 copy.37
  563.9 3.2 copy.46
  567.2 9.8 multiply_reduce_fusion
  577.0 6.6 multiply_convert_fusion
  583.6 2.9 convolution_convert_fusion.4
  586.6 6.2 copy.35
  592.8 3.1 copy.47
  596.0 5.6 fusion.60
  601.6 2.7 fusion.56
  604.3 2.6 copy.38
  606.8 9.3 reduce-scatter.25.cloned.1.call-done
  616.2 1.7 reshape_bitcast_fusion.1
  617.9 2.2 copy.36
  620.1 7.4 convolution_convert_fusion.2
  627.5 110.9 %reduce-scatter.15.cloned.1.call-done = bf16[256,3072]{1,0:T(8,128)(2,1)} async-done(((bf16[1024,3072]{1,0:T(8,128)(2,1)}), bf16[256,3072]{1,0:T(8,128)(2,1)}) %reduce-scatter.15.cloned.1.call-update) | async-done | bytes 1572880 | tf_op jit(solution)/shard_map/reduce_scatter | solution.py:236
  738.5 3.7 convolution_convert_fusion.3
  742.3 8.8 convolution_convert_fusion.1
  751.2 10.6 convolution_convert_fusion
  762.0 7.4 fusion.33
  771.3 21.3 %all-reduce.7.cloned.1.call-done = bf16[256,3072]{1,0:T(8,128)(2,1)} async-done(((bf16[256,3072]{1,0:T(8,128)(2,1)}), bf16[256,3072]{1,0:T(8,128)(2,1)}) %all-reduce.7.cloned.1.call-update) | async-done | bytes 1572880 | tf_op jit(solution)/shard_map/psum | solution.py:259
  792.7 46.8 %reduce-scatter.17.cloned.1.call-done = bf16[256,1024]{1,0:T(8,128)(2,1)} async-done(((bf16[1024,1024]{1,0:T(8,128)(2,1)}), bf16[256,1024]{1,0:T(8,128)(2,1)}) %reduce-scatter.17.cloned.1.call-update) | async-done | bytes 524304 | tf_op jit(solution)/shard_map/reduce_scatter | solution.py:239
  839.5 146.0 %reduce-scatter.19.cloned.1.call-done = bf16[256,4096]{1,0:T(8,128)(2,1)} async-done(((bf16[1024,4096]{1,0:T(8,128)(2,1)}), bf16[256,4096]{1,0:T(8,128)(2,1)}) %reduce-scatter.19.cloned.1.call-update) | async-done | bytes 2097168 | tf_op jit(solution)/shard_map/reduce_scatter | solution.py:242
  985.5 147.6 %reduce-scatter.21.cloned.1.call-done = bf16[1024,1024]{1,0:T(8,128)(2,1)} async-done(((bf16[4096,1024]{1,0:T(8,128)(2,1)}), bf16[1024,1024]{1,0:T(8,128)(2,1)}) %reduce-scatter.21.cloned.1.call-update) | async-done | bytes 2097168 | tf_op jit(solution)/shard_map/reduce_scatter | solution.py:245
  1135.0 11.3 all-reduce
  1146.3 8.6 fusion.25
  1155.0 1.3 fusion.41
  1156.3 0.9 copy.40
  1157.2 18.9 %reduce-scatter.23.cloned.1.call-done = bf16[6,256]{1,0:T(8,128)(2,1)} async-done(((bf16[6,1024]{1,0:T(8,128)(2,1)}), bf16[6,256]{1,0:T(8,128)(2,1)}) %reduce-scatter.23.cloned.1.call-update) | async-done | bytes 3088 | tf_op jit(solution)/shard_map/reduce_scatter | solution.py:251
  1176.2 14.2 %all-reduce.1 = (bf16[2,256]{1,0:T(2,128)(2,1)S(1)}, bf16[6,256]{1,0:T(8,128)(2,1)S(1)}, bf16[1024]{0:T(1024)(128)(2,1)S(1)}) all-reduce(bf16[2,256]{1,0:T(2,128)(2,1)S(1)} %copy.40, bf16[6,256]{1,0:T(8,128)(2,1)} %reduce-scatter.23.cloned.1.call-done, ...), channel_id=1, replica_groups=mesh['rep'=4,'fsdp'=4,'seq'=2] {'rep','seq'}, use_global_device_ids=true, to_apply=%region_25.26 | all-reduce | flops 3072 | bytes 12288 | tf_op jit(solution)/shard_map/psum | solution.py:263
  1192.2 27.3 %all-reduce.9.cloned.1.call-done = bf16[256,3072]{1,0:T(8,128)(2,1)} async-done(((bf16[256,3072]{1,0:T(8,128)(2,1)}), bf16[256,3072]{1,0:T(8,128)(2,1)}) %all-reduce.9.cloned.1.call-update) | async-done | bytes 1572880 | tf_op jit(solution)/shard_map/psum | solution.py:259
  1219.5 3.4 convert_element_type.246
  1223.0 87.3 %all-reduce.11.cloned.1.call-done = (bf16[256,1024]{1,0:T(8,128)(2,1)}, bf16[256,4096]{1,0:T(8,128)(2,1)}, bf16[1024,1024]{1,0:T(8,128)(2,1)}) async-done(((bf16[256,1024]{1,0:T(8,128)(2,1)}, bf16[256,4096]{1,0:T(8,128)(2,1)}, bf16[1024,1024]{1,0:T(8,128)(2,1)}), (bf16[256,1024]{1,0:T(8,128)(2,1)}, bf16[256,4096]{1,0:T(8,128)(2,1)}, bf16[1024,1024]{1,0:T(8,128)(2,1)})) %all-reduce.11.cloned.1.call-update) | async-done | bytes 4718608 | tf_op jit(solution)/shard_map/psum | solution.py:260
  1310.3 2.1 convert_element_type.248
  1312.4 4.2 convert_element_type.250
  1316.7 2.5 convert_element_type.252
  (115 shorter events, 8.7 us)
Async XLA Ops:
  7.2 3.5 copy-start.15
  7.2 3.5 copy-start.17
  7.2 30.4 %copy-start.2 = (bf16[1,296,1024]{2,1,0:T(8,128)(2,1)S(1)}, bf16[1,296,1024]{2,1,0:T(8,128)(2,1)}, u32[]{:S(2)}) copy-start(bf16[1,296,1024]{2,1,0:T(8,128)(2,1)} %param.10) | copy-start | bytes 1818628
  7.2 121.7 %all-gather.9.cloned.1.call-start = ((), (), s32[]{:S(2)}) async-start(), calls=%async_computation.8 | async-start | bytes 7864320 | tf_op jit(solution)/shard_map/all_gather | solution.py:109
  10.6 150.8 %all-gather.17.cloned.1.call-start = ((), (), s32[]{:S(2)}) async-start(), calls=%async_computation.19 | async-start | bytes 1818624 | tf_op jit(solution)/shard_map/all_gather | solution.py:145
  134.0 1.8 copy-start.8
  136.9 2.4 copy-start.12
  137.0 46.9 %all-gather.19.cloned.1.call-start = ((), (), s32[]{:S(2)}) async-start(), calls=%async_computation.20 | async-start | bytes 1818624 | tf_op jit(solution)/shard_map/all_gather | solution.py:144
  139.3 91.9 %all-gather.11.cloned.1.call-start = ((), (), s32[]{:S(2)}) async-start(), calls=%async_computation.9 | async-start | bytes 2621440 | tf_op jit(solution)/shard_map/all_gather | solution.py:110
  140.2 241.2 %all-gather.13.cloned.1.call-start = ((), (), s32[]{:S(2)}) async-start(), calls=%async_computation.10 | async-start | bytes 10485760 | tf_op jit(solution)/shard_map/all_gather | solution.py:111
  144.4 387.0 %all-gather.15.cloned.1.call-start = ((), (), s32[]{:S(2)}) async-start(), calls=%async_computation.11 | async-start | bytes 10485760 | tf_op jit(solution)/shard_map/all_gather | solution.py:112
  148.3 0.7 copy-start.16
  148.3 453.3 %reduce-scatter.27.cloned.1.call-start = ((), (), s32[]{:S(2)}) async-start(), calls=%async_computation.22 | async-start | bytes 1818624
  161.3 24.2 %copy-start.5 = (bf16[296,1024]{0,1:T(8,128)(2,1)}, bf16[296,1024]{0,1:T(8,128)(2,1)S(1)}, u32[]{:S(2)}) copy-start(bf16[296,1024]{0,1:T(8,128)(2,1)S(1)} %copy.32) | copy-start | bytes 1818628
  187.8 4.8 copy-start
  187.8 4.8 copy-start.7
  531.4 9.1 copy-start.18
  540.4 3.1 copy-start.20
  540.5 3.1 copy-start.13
  543.6 1.6 copy-start.10
  544.2 1.0 copy-start.3
  567.1 49.1 %reduce-scatter.25.cloned.1.call-start = ((), (), s32[]{:S(2)}) async-start(), calls=%async_computation.21 | async-start | bytes 1818624
  577.0 6.6 copy-start.6
  583.6 3.0 copy-start.1
  596.0 142.5 %reduce-scatter.15.cloned.1.call-start = ((), (), s32[]{:S(2)}) async-start(), calls=%async_computation.12 | async-start | bytes 7864320 | tf_op jit(solution)/shard_map/reduce_scatter | solution.py:236
  627.5 111.1 %copy-start.4 = (f32[296,1024]{1,0:T(8,128)S(1)}, f32[296,1024]{1,0:T(8,128)}, u32[]{:S(2)}) copy-start(f32[296,1024]{1,0:T(8,128)} %copy-done.3) | copy-start | bytes 3637252
  627.5 165.1 %all-reduce.7.cloned.1.call-start = ((), (), s32[]{:S(2)}) async-start(), calls=%async_computation.13 | async-start | bytes 3145728 | tf_op jit(solution)/shard_map/psum | solution.py:259
  738.5 101.0 %reduce-scatter.17.cloned.1.call-start = ((), (), s32[]{:S(2)}) async-start(), calls=%async_computation.15 | async-start | bytes 2621440 | tf_op jit(solution)/shard_map/reduce_scatter | solution.py:239
  742.2 243.3 %reduce-scatter.19.cloned.1.call-start = ((), (), s32[]{:S(2)}) async-start(), calls=%async_computation.16 | async-start | bytes 10485760 | tf_op jit(solution)/shard_map/reduce_scatter | solution.py:242
  751.1 382.0 %reduce-scatter.21.cloned.1.call-start = ((), (), s32[]{:S(2)}) async-start(), calls=%async_computation.17 | async-start | bytes 10485760 | tf_op jit(solution)/shard_map/reduce_scatter | solution.py:245
  761.8 394.6 %reduce-scatter.29.cloned.1.call-start = ((), (), s32[]{:S(2)}) async-start(), calls=%async_computation.23 | async-start | bytes 327680
  770.4 405.8 %reduce-scatter.23.cloned.1.call-start = ((), (), s32[]{:S(2)}) async-start(), calls=%async_computation.18 | async-start | bytes 20480 | tf_op jit(solution)/shard_map/reduce_scatter | solution.py:251
  771.2 448.3 %all-reduce.9.cloned.1.call-start = ((), (), s32[]{:S(2)}) async-start(), calls=%async_computation.14 | async-start | bytes 3145728 | tf_op jit(solution)/shard_map/psum | solution.py:259
  792.6 517.7 %all-reduce.11.cloned.1.call-start = ((), (), s32[]{:S(2)}) async-start(), calls=%async_computation.24 | async-start | bytes 9437184 | tf_op jit(solution)/shard_map/psum | solution.py:260
  1133.1 0.7 copy-start.19
  1146.3 8.7 copy-start.14
  1146.3 8.7 copy-start.11
  1155.0 21.2 %dynamic-slice-start = ((bf16[4096]{0:T(1024)(128)(2,1)}, u32[]{:T(128)}), bf16[1024]{0:T(1024)(128)(2,1)S(1)}, s32[]{:S(2)}) async-start(bf16[4096]{0:T(1024)(128)(2,1)} %copy-done.14, u32[]{:T(128)} %multiply.49), calls=%async_computation.25 | async-start | bytes 4608
  1312.4 4.3 copy-start.9
Sparse Core Ops, SparseCore 0:
  10.7 118.1 all-gather.8
  137.1 21.4 all-gather.16
  160.7 23.1 all-gather.18
  185.3 45.9 all-gather.10
  233.2 148.2 all-gather.12
  383.5 147.8 all-gather.14
  567.2 20.3 reduce-scatter.26
  596.1 20.0 reduce-scatter.24
  627.6 110.7 reduce-scatter.14
  740.6 51.9 all-reduce.6
  795.6 43.8 reduce-scatter.16
  841.7 143.7 reduce-scatter.18
  987.9 145.1 reduce-scatter.20
  1135.8 20.3 reduce-scatter.28
  1158.9 17.1 reduce-scatter.22
  1178.4 41.0 all-reduce.8
  1223.0 87.2 all-reduce.10
